TPU v7x, 32 devices: a whole 2x2x4 slice. The times are simulated.
32 devices in a mesh: group: 2 (over x), tensor: 8 (over z, y), dp: 2 (over core).
Axes of the slice: x: 2, y: 2, z: 4, core: 2. Of those that a mesh axis runs over, the one named last changes fastest.
Arguments:
- features: bfloat16 [512, 8192], P(('group', 'dp'), 'tensor'), parts along dimension 0, may hold values from -64 to 64
- cotangent: bfloat16 [512, 8192], P(('group', 'dp'), 'tensor'), parts along dimension 0, may hold values from -64 to 64
- token_tenant: int32 [512], P(('group', 'dp')), parts along dimension 0, may hold values from 0 to 15
- owner_device: int32 [32], P('group'), parts along dimension 0, may hold values from 0 to 15, each once
- frozen_weight: bfloat16 [8192, 8192], P('tensor'), may hold values from -0.09375 to 0.09375
- adapter_down: bfloat16 [32, 16, 8192], P('group', None, 'tensor'), parts along dimension 0, may hold values from -0.0625 to 0.0625
- adapter_up: bfloat16 [32, 16, 8192], P('group', None, 'tensor'), parts along dimension 0, may hold values from -0.29882812 to 0.29882812
- momentum_down: float32 [32, 16, 8192], P(('group', 'tensor', 'dp')), parts along dimension 0, may hold values from -12 to 12
- momentum_up: float32 [32, 16, 8192], P(('group', 'tensor', 'dp')), parts along dimension 0, may hold values from -3 to 3
- variance_down: float32 [32, 16, 8192], P(('group', 'tensor', 'dp')), parts along dimension 0, may hold values from 0.3 to 3
- variance_up: float32 [32, 16, 8192], P(('group', 'tensor', 'dp')), parts along dimension 0, may hold values from 0.02 to 0.2
Outputs:
- projected: bfloat16 [512, 8192], P(('group', 'dp'), 'tensor'), parts along dimension 0
- updated_down: bfloat16 [32, 16, 8192], P('group', None, 'tensor'), parts along dimension 0
- updated_up: bfloat16 [32, 16, 8192], P('group', None, 'tensor'), parts along dimension 0
- mean_down: float32 [32, 16, 8192], P(('group', 'tensor', 'dp')), parts along dimension 0
- mean_up: float32 [32, 16, 8192], P(('group', 'tensor', 'dp')), parts along dimension 0
- power_down: float32 [32, 16, 8192], P(('group', 'tensor', 'dp')), parts along dimension 0
- power_up: float32 [32, 16, 8192], P(('group', 'tensor', 'dp')), parts along dimension 0
There are 2 independent parts, one for each index of `group`. A program takes and returns all parts, laid end to end along the dimension named above; an argument that names none is the same for every part. Nothing has to cross between parts.
Inputs may be any that keep to these rules, and one draw needn't show every extreme that they name: Tenant t belongs to the device whose index along tensor+dp (dp fastest) is owner_device[t]; every index appears once.
All inputs are finite; a program needn't handle non-finite values.
Results may differ from a plain program's by a relative error of at most 0.0014.
The roundings to bfloat16 on the way count: a program that leaves them out, or rounds other values in their place, can miss the bound.
Values sent between devices are 32-bit elements; how exact they have to be, the bound alone decides.
A program may use at most 128 MiB of HBM per device.

v0:
```python
import jax
import jax.numpy as jnp
from jax import lax
from jax.sharding import PartitionSpec as P

adapter_scale = 2.0
clip_norm = 12000.0
learn_rate = 0.004
beta_one = 0.9
beta_two = 0.999
adam_eps = 1e-08
correct_one = 1.0 - beta_one**20
correct_two = 1.0 - beta_two**20


def tenant_mask(token_tenant, tenants, lowrank):
    columns = lax.broadcasted_iota(jnp.int32, (1, tenants * lowrank), 1) // lowrank
    return token_tenant[:, None] == columns


def rank_fold(tenants, lowrank):
    row_index = lax.broadcasted_iota(jnp.int32, (tenants * lowrank, lowrank), 0) % lowrank
    col_index = lax.broadcasted_iota(jnp.int32, (tenants * lowrank, lowrank), 1)
    return (row_index == col_index).astype(jnp.float32)


def select_rank(scores, token_mask, folding):
    picked = jnp.where(token_mask, scores, jnp.zeros_like(scores))
    return jnp.dot(
        picked, folding, precision=lax.Precision.HIGHEST, preferred_element_type=jnp.float32
    )


def spread_rank(values, token_mask, tenants):
    scaled = (adapter_scale * values).astype(jnp.bfloat16)
    tiled_rank = jnp.tile(scaled, (1, tenants))
    return jnp.where(token_mask, tiled_rank, jnp.zeros_like(tiled_rank))


def owner_order(owner_device):
    total = owner_device.shape[0]
    slot_index = lax.broadcasted_iota(jnp.int32, (total, total), 0)
    tenant_index = lax.broadcasted_iota(jnp.int32, (total, total), 1)
    return jnp.sum(jnp.where(owner_device[None, :] == slot_index, tenant_index, 0), axis=1)


def adam_step(gradient, factor, moment, square):
    clipped = gradient * factor
    moment_next = beta_one * moment + (1.0 - beta_one) * clipped
    square_next = beta_two * square + (1.0 - beta_two) * clipped * clipped
    change = (
        learn_rate * (moment_next / correct_one) / (jnp.sqrt(square_next / correct_two) + adam_eps)
    )
    return (moment_next, square_next, change)


def frozen_blocks(features, frozen_weight, width_shard, blocks):
    columns = frozen_weight
    columns = columns.reshape(frozen_weight.shape[0], blocks, width_shard)
    return jnp.einsum("ti,ibc->btc", features, columns, preferred_element_type=jnp.float32)


def on_device(
    features,
    cotangent,
    token_tenant,
    owner_device,
    frozen_weight,
    adapter_down,
    adapter_up,
    momentum_down,
    momentum_up,
    variance_down,
    variance_up,
):
    tokens = features.shape[0]
    tenants, lowrank, width_shard = adapter_down.shape
    parts_tensor = lax.axis_size("tensor")
    parts_dp = lax.axis_size("dp")
    token_mask = tenant_mask(token_tenant, tenants, lowrank)
    folding = rank_fold(tenants, lowrank)
    down_flat = adapter_down.reshape(tenants * lowrank, width_shard)
    up_flattened = adapter_up.reshape(tenants * lowrank, width_shard)
    contract = (((1,), (1,)), ((), ()))
    down_part = select_rank(
        lax.dot_general(features, down_flat, contract, preferred_element_type=jnp.float32),
        token_mask,
        folding,
    )
    up_part = select_rank(
        lax.dot_general(cotangent, up_flattened, contract, preferred_element_type=jnp.float32),
        token_mask,
        folding,
    )
    blocks = lax.axis_size("tensor") * tokens // tokens
    result = frozen_blocks(features, frozen_weight, width_shard, blocks)
    frozen_result = lax.psum_scatter(
        result.reshape(blocks * tokens, width_shard), "tensor", scatter_dimension=0, tiled=True
    )
    down_sum, up_sum = lax.psum((down_part, up_part), "tensor")
    down_scattered = spread_rank(down_sum, token_mask, tenants)
    up_scattered = spread_rank(up_sum, token_mask, tenants)
    adapter_result = jnp.dot(down_scattered, up_flattened, preferred_element_type=jnp.float32)
    projected = (frozen_result + adapter_result).astype(jnp.bfloat16)
    outer_product = (((0,), (0,)), ((), ()))
    down_gradient = lax.dot_general(
        up_scattered, features, outer_product, preferred_element_type=jnp.float32
    )
    up_gradient = lax.dot_general(
        down_scattered, cotangent, outer_product, preferred_element_type=jnp.float32
    )
    down_gradient = down_gradient.reshape(tenants, lowrank, width_shard)
    up_gradient = up_gradient.reshape(tenants, lowrank, width_shard)
    slot_tenant = owner_order(owner_device)
    half_index = lax.broadcasted_iota(jnp.int32, (tenants,), 0)
    slot_index = half_index % parts_tensor * parts_dp + half_index // parts_tensor
    half_tenant = jnp.take(slot_tenant, slot_index, axis=0)
    down_halves = jnp.take(down_gradient, half_tenant, axis=0)
    up_halves = jnp.take(up_gradient, half_tenant, axis=0)
    summed = (
        lax.psum_scatter(down_halves, "dp", scatter_dimension=0, tiled=True),
        lax.psum_scatter(up_halves, "dp", scatter_dimension=0, tiled=True),
    )
    own_down, own_up = (
        lax.all_to_all(summed[0], "tensor", split_axis=0, concat_axis=2, tiled=True),
        lax.all_to_all(summed[1], "tensor", split_axis=0, concat_axis=2, tiled=True),
    )
    squares = jnp.sum(own_down * own_down) + jnp.sum(own_up * own_up)
    factor = clip_norm / jnp.maximum(jnp.sqrt(squares), clip_norm)
    mean_down, power_down, change_down = adam_step(own_down, factor, momentum_down, variance_down)
    mean_up, power_up, change_up = adam_step(own_up, factor, momentum_up, variance_up)
    pieces = (
        lax.all_to_all(change_down, ("tensor", "dp"), split_axis=2, concat_axis=0, tiled=True),
        lax.all_to_all(change_up, ("tensor", "dp"), split_axis=2, concat_axis=0, tiled=True),
    )
    joined = (
        lax.all_gather(pieces[0], "dp", axis=2, tiled=True),
        lax.all_gather(pieces[1], "dp", axis=2, tiled=True),
    )
    back_down = jnp.take(joined[0], owner_device, axis=0)
    back_up = jnp.take(joined[1], owner_device, axis=0)
    updated_down = (adapter_down.astype(jnp.float32) - back_down).astype(jnp.bfloat16)
    updated_up = (adapter_up.astype(jnp.float32) - back_up).astype(jnp.bfloat16)
    return (projected, updated_down, updated_up, mean_down, mean_up, power_down, power_up)


def solution(mesh):
    in_specs = (
        P(("group", "dp"), "tensor"),
        P(("group", "dp"), "tensor"),
        P(("group", "dp")),
        P("group"),
        P("tensor", None),
        P("group", None, "tensor"),
        P("group", None, "tensor"),
        P(("group", "tensor", "dp"), None, None),
        P(("group", "tensor", "dp"), None, None),
        P(("group", "tensor", "dp"), None, None),
        P(("group", "tensor", "dp"), None, None),
    )
    out_specs = (
        P(("group", "dp"), "tensor"),
        P("group", None, "tensor"),
        P("group", None, "tensor"),
        P(("group", "tensor", "dp"), None, None),
        P(("group", "tensor", "dp"), None, None),
        P(("group", "tensor", "dp"), None, None),
        P(("group", "tensor", "dp"), None, None),
    )
    return jax.shard_map(
        on_device, mesh=mesh, in_specs=in_specs, out_specs=out_specs, check_vma=False
    )
```

profile of v0, /device:TPU:0, one launch (start us, length us, event | category | flops | bytes accessed | tf_op | source)
XLA Modules:
  0.0 376.7 jit_solution(10851005240872450794)
XLA Ops:
  8.1 1.5 convolution_select_fusion
  9.6 1.4 convolution_select_fusion.1
  11.0 0.4 fusion.14
  11.4 0.4 fusion.15
  11.8 38.9 %all-reduce = (f32[128,16]{0,1:T(8,128)S(1)}, f32[128,16]{0,1:T(8,128)S(1)}) all-reduce(f32[128,16]{0,1:T(8,128)S(1)} %fusion.15, f32[128,16]{0,1:T(8,128)S(1)} %fusion.14), channel_id=1, replica_groups=mesh['group'=2,'tensor'=8,'dp'=2] {'tensor'}, use_global_device_ids=true, to_apply=%region_1.2 | all-reduce | flops 4096 | bytes 32768 | tf_op jit(solution)/shard_map/psum | solution.py:100
  50.9 0.7 fusion.17
  51.8 0.3 fusion.11
  52.1 0.1 select_reduce_fusion
  52.2 0.7 gather_fusion
  52.9 0.1 copy.44
  53.0 0.3 fusion.9
  53.3 0.6 gather_fusion.1
  53.9 0.6 gather_fusion.2
  54.6 1.6 broadcast_select_fusion
  56.3 0.7 reduce-scatter.6.cloned.1.call-update
  57.0 5.0 %reduce-scatter.8.cloned.1.call-done = f32[8,16,1024]{2,1,0:T(8,128)} async-done(((f32[16,16,1024]{2,1,0:T(8,128)}), f32[8,16,1024]{2,1,0:T(8,128)}) %reduce-scatter.8.cloned.1.call-update) | async-done | bytes 524304 | tf_op jit(solution)/shard_map/reduce_scatter | solution.py:122
  62.0 5.8 %all-to-all-start.1 = ((f32[8,16,1024]{2,1,0:T(8,128)}), f32[8,16,1024]{2,1,0:T(8,128)S(1)}, u32[]{:S(2)}, u32[]{:S(2)}) async-start(f32[8,16,1024]{2,1,0:T(8,128)} %reduce-scatter.8.cloned.1.call-done), calls=%async_computation.4 | async-start | bytes 1048576 | tf_op jit(solution)/shard_map/all_to_all | solution.py:126
  67.8 6.0 %reduce-scatter.6.cloned.1.call-done = f32[8,16,1024]{2,1,0:T(8,128)} async-done(((f32[16,16,1024]{2,1,0:T(8,128)}), f32[8,16,1024]{2,1,0:T(8,128)}) %reduce-scatter.6.cloned.1.call-update) | async-done | bytes 524304 | tf_op jit(solution)/shard_map/reduce_scatter | solution.py:121
  73.9 8.9 %all-to-all-done.1 = f32[8,16,1024]{2,1,0:T(8,128)S(1)} async-done(((f32[8,16,1024]{2,1,0:T(8,128)}), f32[8,16,1024]{2,1,0:T(8,128)S(1)}, u32[]{:S(2)}, u32[]{:S(2)}) %all-to-all-start.1) | async-done | bytes 524320 | tf_op jit(solution)/shard_map/all_to_all | solution.py:126
  82.7 3.6 all-to-all-start
  86.4 0.7 multiply_reduce_fusion
  87.1 13.9 %all-to-all-done = f32[8,16,1024]{2,1,0:T(8,128)S(1)} async-done(((f32[8,16,1024]{2,1,0:T(8,128)}), f32[8,16,1024]{2,1,0:T(8,128)S(1)}, u32[]{:S(2)}, u32[]{:S(2)}) %all-to-all-start) | async-done | bytes 524320 | tf_op jit(solution)/shard_map/all_to_all | solution.py:125
  101.0 0.7 multiply_reduce_fusion.1
  103.3 1.3 add_divide_fusion.1
  104.5 6.4 %copy.46 = f32[1,16,8192]{1,0,2:T(1,128)} copy(f32[1,16,8192]{2,1,0:T(8,128)S(1)} %get-tuple-element.13) | data formatting | bytes 1048576 | tf_op jit(solution)/shard_map/div | solution.py:52
  111.0 0.5 broadcast.462
  111.5 38.4 %reduce.8 = f32[8192,16]{1,0:T(8,128)} reduce(f32[8192,1,16]{2,1,0:T(1,128)} %bitcast.66, f32[]{:T(128)} %broadcast.462), dimensions={1}, to_apply=%bitcast.51.reduce_sub_computation | reduce | bytes 1048580
  149.9 4.2 %reshape.313 = f32[16,1,8192]{2,1,0:T(1,128)} reshape(f32[8192,16]{1,0:T(8,128)} %reduce.8) | data formatting | bytes 1048576
  154.1 3.7 all-to-all-start.2
  157.8 0.2 all-gather.5.cloned.1.call-start
  158.2 13.9 %all-to-all-done.2 = f32[16,1,8192]{2,1,0:T(1,128)S(1)} async-done(((f32[16,1,8192]{2,1,0:T(1,128)}), f32[16,1,8192]{2,1,0:T(1,128)S(1)}, u32[]{:S(2)}, u32[]{:S(2)}) %all-to-all-start.2) | async-done | bytes 524320 | tf_op jit(solution)/shard_map/all_to_all | solution.py:133
  172.1 1.9 reduce.9
  174.0 9.3 %reshape.314 = f32[8192,1,16]{2,1,0:T(1,128)} reshape(f32[16,8192]{1,0:T(8,128)S(1)} %reduce.9) | data formatting | bytes 1048576
  183.3 3.5 copy.48
  186.9 1.3 add_divide_fusion
  188.2 6.4 %copy.50 = f32[1,16,8192]{1,0,2:T(1,128)} copy(f32[1,16,8192]{2,1,0:T(8,128)S(1)} %get-tuple-element.10) | data formatting | bytes 1048576 | tf_op jit(solution)/shard_map/div | solution.py:52
  194.6 38.4 %reduce.6 = f32[8192,16]{1,0:T(8,128)} reduce(f32[8192,1,16]{2,1,0:T(1,128)} %bitcast.67, f32[]{:T(128)} %broadcast.462), dimensions={1}, to_apply=%bitcast.53.reduce_sub_computation | reduce | bytes 1048580
  233.0 3.5 reshape.315
  236.5 18.4 %all_to_all.54 = f32[16,1,8192]{2,1,0:T(1,128)S(1)} all-to-all(f32[16,1,8192]{2,1,0:T(1,128)S(1)} %reshape.315), channel_id=1, replica_groups=mesh['group'=2,'tensor'=8,'dp'=2] {'tensor','dp'}, dimensions={0} | all-to-all | bytes 1048576 | tf_op jit(solution)/shard_map/all_to_all | solution.py:134
  254.9 1.9 reduce.7
  256.8 9.3 %reshape.316 = f32[8192,1,16]{2,1,0:T(1,128)} reshape(f32[16,8192]{1,0:T(8,128)S(1)} %reduce.7) | data formatting | bytes 1048576
  266.0 3.5 copy.52
  269.6 10.1 %fusion = f32[8,1024,128]{1,2,0:T(8,128)} fusion(bf16[128,8,8,1024]{3,2,1,0:T(8,128)(2,1)} %bitcast.81, bf16[128,1024]{1,0:T(8,128)(2,1)S(1)} %copy-done), kind=kOutput, calls=%fused_computation.5 | convolution fusion | flops 2147483648 | bytes 21233664 | tf_op jit(solution)/shard_map/ti,ibc->btc/dot_general | solution.py:60
  279.9 1.9 gather_fusion.3
  281.8 1.8 gather_fusion.4
  283.7 1.4 fusion.5
  285.1 82.4 %reduce-scatter.4.cloned.1.call-done = f32[128,1024]{1,0:T(8,128)} async-done(((f32[1024,1024]{1,0:T(8,128)}), f32[128,1024]{1,0:T(8,128)}) %reduce-scatter.4.cloned.1.call-update) | async-done | bytes 524304 | tf_op jit(solution)/shard_map/reduce_scatter | solution.py:97
  367.5 2.1 fusion.4
  (52 shorter events, 0.9 us)
Async XLA Ops:
  8.0 1.6 copy-start
  8.0 45.0 %copy-start.3 = (bf16[128,1024]{1,0:T(8,128)(2,1)S(1)}, bf16[128,1024]{1,0:T(8,128)(2,1)}, u32[]{:S(2)}) copy-start(bf16[128,1024]{1,0:T(8,128)(2,1)} %param.14) | copy-start | bytes 786436
  8.0 44.1 %copy-start.9 = (s32[16]{0:T(128)S(1)}, s32[16]{0:T(128)}, u32[]{:S(2)}) copy-start(s32[16]{0:T(128)} %param.16) | copy-start | bytes 196
  8.0 54.0 %reduce-scatter.8.cloned.1.call-start = ((), (), s32[]{:S(2)}) async-start(), calls=%async_computation.9 | async-start | bytes 1572864 | tf_op jit(solution)/shard_map/reduce_scatter | solution.py:122
  56.2 47.1 %copy-start.4 = (f32[1,16,8192]{2,1,0:T(8,128)S(1)}, f32[1,16,8192]{2,1,0:T(8,128)}, u32[]{:S(2)}) copy-start(f32[1,16,8192]{2,1,0:T(8,128)} %param.20) | copy-start | bytes 1572868
  56.2 47.1 %copy-start.5 = (f32[1,16,8192]{2,1,0:T(8,128)S(1)}, f32[1,16,8192]{2,1,0:T(8,128)}, u32[]{:S(2)}) copy-start(f32[1,16,8192]{2,1,0:T(8,128)} %param.22) | copy-start | bytes 1572868
  56.2 17.7 %reduce-scatter.6.cloned.1.call-start = ((), (), s32[]{:S(2)}) async-start(), calls=%async_computation.8 | async-start | bytes 1572864 | tf_op jit(solution)/shard_map/reduce_scatter | solution.py:121
  62.0 20.7 %all-to-all-start.1 = ((f32[8,16,1024]{2,1,0:T(8,128)}), f32[8,16,1024]{2,1,0:T(8,128)S(1)}, u32[]{:S(2)}, u32[]{:S(2)}) async-start(f32[8,16,1024]{2,1,0:T(8,128)} %reduce-scatter.8.cloned.1.call-done), calls=%async_computation.4 | async-start | bytes 1048576 | tf_op jit(solution)/shard_map/all_to_all | solution.py:126
  82.7 18.3 %all-to-all-start = ((f32[8,16,1024]{2,1,0:T(8,128)}), f32[8,16,1024]{2,1,0:T(8,128)S(1)}, u32[]{:S(2)}, u32[]{:S(2)}) async-start(f32[8,16,1024]{2,1,0:T(8,128)} %reduce-scatter.6.cloned.1.call-done), calls=%async_computation.2 | async-start | bytes 1048576 | tf_op jit(solution)/shard_map/all_to_all | solution.py:125
  154.1 18.0 %all-to-all-start.2 = ((f32[16,1,8192]{2,1,0:T(1,128)}), f32[16,1,8192]{2,1,0:T(1,128)S(1)}, u32[]{:S(2)}, u32[]{:S(2)}) async-start(f32[16,1,8192]{2,1,0:T(1,128)} %reshape.313), calls=%async_computation.5 | async-start | bytes 1048576 | tf_op jit(solution)/shard_map/all_to_all | solution.py:133
  157.8 122.0 %all-gather.5.cloned.1.call-start = ((), (), s32[]{:S(2)}) async-start(), calls=%async_computation.10 | async-start | bytes 1572864 | tf_op jit(solution)/shard_map/all_gather | solution.py:137
  174.0 12.9 %copy-start.6 = (f32[1,16,8192]{2,1,0:T(8,128)S(1)}, f32[1,16,8192]{2,1,0:T(8,128)}, u32[]{:S(2)}) copy-start(f32[1,16,8192]{2,1,0:T(8,128)} %param.21) | copy-start | bytes 1572868
  174.0 12.9 %copy-start.7 = (f32[1,16,8192]{2,1,0:T(8,128)S(1)}, f32[1,16,8192]{2,1,0:T(8,128)}, u32[]{:S(2)}) copy-start(f32[1,16,8192]{2,1,0:T(8,128)} %param.23) | copy-start | bytes 1572868
  186.8 95.0 %all-gather.7.cloned.1.call-start = ((), (), s32[]{:S(2)}) async-start(), calls=%async_computation.11 | async-start | bytes 1572864 | tf_op jit(solution)/shard_map/all_gather | solution.py:138
  269.6 97.9 %reduce-scatter.4.cloned.1.call-start = ((), (), s32[]{:S(2)}) async-start(), calls=%async_computation.7 | async-start | bytes 4718592 | tf_op jit(solution)/shard_map/reduce_scatter | solution.py:97
  279.7 3.9 %copy-start.1 = (bf16[16,16,1024]{2,1,0:T(8,128)(2,1)S(1)}, bf16[16,16,1024]{2,1,0:T(8,128)(2,1)}, u32[]{:S(2)}) copy-start(bf16[16,16,1024]{2,1,0:T(8,128)(2,1)} %param.19) | copy-start | bytes 1572868
  279.7 3.9 %copy-start.2 = (bf16[16,16,1024]{2,1,0:T(8,128)(2,1)S(1)}, bf16[16,16,1024]{2,1,0:T(8,128)(2,1)}, u32[]{:S(2)}) copy-start(bf16[16,16,1024]{2,1,0:T(8,128)(2,1)} %param.18) | copy-start | bytes 1572868
  279.9 87.6 %copy-start.8 = (s32[128]{0:T(128)S(1)}, s32[128]{0:T(128)}, u32[]{:S(2)}) copy-start(s32[128]{0:T(128)} %param.15) | copy-start | bytes 1540
Sparse Core Ops, SparseCore 0:
  56.3 5.6 reduce-scatter.7
  64.2 9.5 reduce-scatter.5
  186.9 8.5 all-gather.4
  269.7 8.5 all-gather.6
Sparse Core Ops, SparseCore 1:
  279.9 87.5 reduce-scatter.3
where the time goes:
time: 378 us; the launch traced here: 377 us
  waiting for transfers between devices  131 us (35%)
  other arithmetic  88.7 us (23%)
  blocking collectives  57.2 us (15%)
  local copies, waits for them, and re-layouts  52.8 us (14%)
  between operations  17 us (4%)
  matrix products  16.4 us (4%)
  starting transfers between devices  13.6 us (4%)
    reduce_scatter x1, waiting for transfers between devices, on_device(): lax.psum_scatter(result.reshape(blocks * tokens, width_shard), 'tensor',...  82.4 us
    unnamed x4, other arithmetic  76.9 us
    psum x1, blocking collectives, on_device(): down_sum, up_sum = lax.psum((down_part, up_part), 'tensor')  38.9 us
    unnamed x25, local copies, waits for them, and re-layouts  26.8 us
    all_to_all x1, blocking collectives, on_device(): lax.all_to_all(change_up, ('tensor', 'dp'), split_axis=2, concat_axis=0,...  18.4 us
    all_to_all x1, waiting for transfers between devices, on_device(): lax.all_to_all(summed[0], 'tensor', split_axis=0, concat_axis=2, tiled=True)  13.9 us
    all_to_all x1, waiting for transfers between devices, on_device(): lax.all_to_all(change_down, ('tensor', 'dp'), split_axis=2, concat_axis=0...  13.9 us
    div x2, local copies, waits for them, and re-layouts, adam_step(): learn_rate * (moment_next / correct_one)  12.8 us
  transfers between devices with their start and end apart: 8, of which 6 were waited for; matrix products, arithmetic and copies ran while one was open for 21% of the time, Pallas kernels for 0%

commit v1 on v0

--- a/solution.py
+++ b/solution.py
@@ -11,6 +11,13 @@
 adam_eps = 1e-08
 correct_one = 1.0 - beta_one**20
 correct_two = 1.0 - beta_two**20
+
+
+def swap_blocks(block, mesh_axis, split, join):
+    size = lax.axis_size(mesh_axis)
+    blocks = jnp.stack(jnp.split(block, size, axis=split), axis=0)
+    blocks = lax.all_to_all(blocks, mesh_axis, split_axis=0, concat_axis=0)
+    return jnp.concatenate(blocks, axis=join)
 
 
 def tenant_mask(token_tenant, tenants, lowrank):
@@ -131,7 +138,7 @@
     mean_up, power_up, change_up = adam_step(own_up, factor, momentum_up, variance_up)
     pieces = (
         lax.all_to_all(change_down, ("tensor", "dp"), split_axis=2, concat_axis=0, tiled=True),
-        lax.all_to_all(change_up, ("tensor", "dp"), split_axis=2, concat_axis=0, tiled=True),
+        swap_blocks(change_up, ("tensor", "dp"), 2, 0),
     )
     joined = (
         lax.all_gather(pieces[0], "dp", axis=2, tiled=True),

time: 378 us -> 316 us (0.84)
  other arithmetic: 88.7 us -> 50.2 us
  local copies, waits for them, and re-layouts: 52.8 us -> 30.1 us
    unnamed x4 -> x3, other arithmetic: 76.9 us -> 38.5 us
    unnamed x25 -> x32, local copies, waits for them, and re-layouts: 26.8 us -> 14.1 us
    div x2 -> x1, local copies, waits for them, and re-layouts: 12.8 us -> 6.39 us  [adam_step(): learn_rate * (moment_next / correct_one)]
  transfers between devices with their start and end apart: 8 -> 8, of which waited for: 6 -> 6; matrix products, arithmetic and copies ran while one was open for 21% -> 6% of each run, Pallas kernels for 0% -> 0%
where the time goes in v1:
time: 316 us; the launch traced here: 315 us
  waiting for transfers between devices  130 us (41%)
  blocking collectives  57.3 us (18%)
  other arithmetic  50.2 us (16%)
  local copies, waits for them, and re-layouts  30.1 us (10%)
  matrix products  17.3 us (5%)
  between operations  17 us (5%)
  starting transfers between devices  13.6 us (4%)
    reduce_scatter x1, waiting for transfers between devices, on_device(): lax.psum_scatter(result.reshape(blocks * tokens, width_shard), 'tensor',...  82.4 us
    psum x1, blocking collectives, on_device(): down_sum, up_sum = lax.psum((down_part, up_part), 'tensor')  38.9 us
    unnamed x3, other arithmetic  38.5 us
    all_to_all x1, blocking collectives, swap_blocks(): blocks = lax.all_to_all(blocks, mesh_axis, split_axis=0, concat_axis=0)  18.5 us
    unnamed x32, local copies, waits for them, and re-layouts  14.1 us
    all_to_all x1, waiting for transfers between devices, on_device(): lax.all_to_all(summed[0], 'tensor', split_axis=0, concat_axis=2, tiled=True)  13.9 us
    all_to_all x1, waiting for transfers between devices, on_device(): lax.all_to_all(change_down, ('tensor', 'dp'), split_axis=2, concat_axis=0...  12.4 us
    dot_general x1, matrix products, frozen_blocks(): jnp.einsum('ti,ibc->btc', features, columns, preferred_element_type=jnp.f...  10.2 us
  transfers between devices with their start and end apart: 8, of which 6 were waited for; matrix products, arithmetic and copies ran while one was open for 6% of the time, Pallas kernels for 0%

profile of v1, /device:TPU:0, one launch (start us, length us, event | category | flops | bytes accessed | tf_op | source)
XLA Modules:
  0.0 315.2 jit_solution(526088851736116084)
XLA Ops:
  8.1 1.4 convolution_select_fusion
  9.5 1.4 convolution_select_fusion.1
  10.9 0.4 fusion.14
  11.3 0.4 fusion.15
  11.7 38.9 %all-reduce = (f32[128,16]{0,1:T(8,128)S(1)}, f32[128,16]{0,1:T(8,128)S(1)}) all-reduce(f32[128,16]{0,1:T(8,128)S(1)} %fusion.15, f32[128,16]{0,1:T(8,128)S(1)} %fusion.14), channel_id=1, replica_groups=mesh['group'=2,'tensor'=8,'dp'=2] {'tensor'}, use_global_device_ids=true, to_apply=%region_1.2 | all-reduce | flops 4096 | bytes 32768 | tf_op jit(solution)/shard_map/psum | solution.py:107
  50.6 0.1 copy.41
  50.7 0.1 copy.39
  50.8 0.7 fusion.17
  51.6 0.1 copy.40
  51.7 0.3 fusion.11
  52.0 0.8 select_reduce_fusion
  52.8 0.7 gather_fusion
  53.5 0.1 copy.42
  53.6 1.2 fusion.9
  54.8 0.6 gather_fusion.1
  55.5 0.6 gather_fusion.2
  56.1 1.6 broadcast_select_fusion
  57.7 0.0 reduce-scatter.6.cloned.1.call-start
  57.8 0.7 reduce-scatter.6.cloned.1.call-update
  58.5 5.1 %reduce-scatter.8.cloned.1.call-done = f32[8,16,1024]{2,1,0:T(8,128)} async-done(((f32[16,16,1024]{2,1,0:T(8,128)}), f32[8,16,1024]{2,1,0:T(8,128)}) %reduce-scatter.8.cloned.1.call-update) | async-done | bytes 524304 | tf_op jit(solution)/shard_map/reduce_scatter | solution.py:129
  63.5 5.8 %all-to-all-start.1 = ((f32[8,16,1024]{2,1,0:T(8,128)}), f32[8,16,1024]{2,1,0:T(8,128)S(1)}, u32[]{:S(2)}, u32[]{:S(2)}) async-start(f32[8,16,1024]{2,1,0:T(8,128)} %reduce-scatter.8.cloned.1.call-done), calls=%async_computation.4 | async-start | bytes 1048576 | tf_op jit(solution)/shard_map/all_to_all | solution.py:133
  69.3 6.0 %reduce-scatter.6.cloned.1.call-done = f32[8,16,1024]{2,1,0:T(8,128)} async-done(((f32[16,16,1024]{2,1,0:T(8,128)}), f32[8,16,1024]{2,1,0:T(8,128)}) %reduce-scatter.6.cloned.1.call-update) | async-done | bytes 524304 | tf_op jit(solution)/shard_map/reduce_scatter | solution.py:128
  75.4 8.9 %all-to-all-done.1 = f32[8,16,1024]{2,1,0:T(8,128)S(1)} async-done(((f32[8,16,1024]{2,1,0:T(8,128)}), f32[8,16,1024]{2,1,0:T(8,128)S(1)}, u32[]{:S(2)}, u32[]{:S(2)}) %all-to-all-start.1) | async-done | bytes 524320 | tf_op jit(solution)/shard_map/all_to_all | solution.py:133
  84.2 3.6 %all-to-all-start = ((f32[8,16,1024]{2,1,0:T(8,128)}), f32[8,16,1024]{2,1,0:T(8,128)S(1)}, u32[]{:S(2)}, u32[]{:S(2)}) async-start(f32[8,16,1024]{2,1,0:T(8,128)} %reduce-scatter.6.cloned.1.call-done), calls=%async_computation.2 | async-start | bytes 1048576 | tf_op jit(solution)/shard_map/all_to_all | solution.py:132
  87.9 0.7 multiply_reduce_fusion
  88.6 13.9 %all-to-all-done = f32[8,16,1024]{2,1,0:T(8,128)S(1)} async-done(((f32[8,16,1024]{2,1,0:T(8,128)}), f32[8,16,1024]{2,1,0:T(8,128)S(1)}, u32[]{:S(2)}, u32[]{:S(2)}) %all-to-all-start) | async-done | bytes 524320 | tf_op jit(solution)/shard_map/all_to_all | solution.py:132
  102.5 0.7 multiply_reduce_fusion.1
  104.8 2.5 add_divide_fusion.1
  107.2 6.4 %copy.44 = f32[1,16,8192]{1,0,2:T(1,128)} copy(f32[1,16,8192]{2,1,0:T(8,128)S(1)} %get-tuple-element.13) | data formatting | bytes 1048576 | tf_op jit(solution)/shard_map/div | solution.py:59
  113.6 0.5 broadcast.462
  114.2 38.4 %reduce.6 = f32[8192,16]{1,0:T(8,128)} reduce(f32[8192,1,16]{2,1,0:T(1,128)} %bitcast.125, f32[]{:T(128)} %broadcast.462), dimensions={1}, to_apply=%bitcast.113.reduce_sub_computation | reduce | bytes 1048580
  152.6 4.2 %reshape.317 = f32[16,1,8192]{2,1,0:T(1,128)} reshape(f32[8192,16]{1,0:T(8,128)} %reduce.6) | data formatting | bytes 1048576
  156.8 3.7 %all-to-all-start.2 = ((f32[16,1,8192]{2,1,0:T(1,128)}), f32[16,1,8192]{2,1,0:T(1,128)S(1)}, u32[]{:S(2)}, u32[]{:S(2)}) async-start(f32[16,1,8192]{2,1,0:T(1,128)} %reshape.317), calls=%async_computation.5 | async-start | bytes 1048576 | tf_op jit(solution)/shard_map/all_to_all | solution.py:140
  160.5 0.2 all-gather.5.cloned.1.call-start
  160.9 1.3 add_divide_fusion
  162.3 12.4 %all-to-all-done.2 = f32[16,1,8192]{2,1,0:T(1,128)S(1)} async-done(((f32[16,1,8192]{2,1,0:T(1,128)}), f32[16,1,8192]{2,1,0:T(1,128)S(1)}, u32[]{:S(2)}, u32[]{:S(2)}) %all-to-all-start.2) | async-done | bytes 524320 | tf_op jit(solution)/shard_map/all_to_all | solution.py:140
  174.8 1.9 reduce.7
  176.7 9.3 %reshape.318 = f32[8192,1,16]{2,1,0:T(1,128)} reshape(f32[16,8192]{1,0:T(8,128)S(1)} %reduce.7) | data formatting | bytes 1048576
  186.0 3.5 %copy.46 = f32[1,16,16,512]{3,1,2,0:T(8,128)} copy(f32[1,16,16,512]{1,3,2,0:T(8,128)} %bitcast.124) | data formatting | bytes 1048576 | tf_op jit(solution)/shard_map/all_to_all | solution.py:140
  189.5 0.0 all-gather.7.cloned.1.call-start
  189.6 18.5 %all_to_all.41 = f32[16,1,16,512]{3,2,1,0:T(8,128)} all-to-all(f32[16,1,16,512]{3,2,1,0:T(8,128)S(1)} %fusion.26), channel_id=1, replica_groups=mesh['group'=2,'tensor'=8,'dp'=2] {'tensor','dp'}, dimensions={0} | all-to-all | bytes 1048576 | tf_op jit(solution)/shard_map/all_to_all | solution.py:19
  208.1 0.0 reduce-scatter.4.cloned.1.call-start
  208.1 10.2 %fusion = f32[8,1024,128]{1,2,0:T(8,128)} fusion(bf16[128,8,8,1024]{3,2,1,0:T(8,128)(2,1)} %bitcast.138, bf16[128,1024]{1,0:T(8,128)(2,1)S(1)} %copy-done), kind=kOutput, calls=%fused_computation.5 | convolution fusion | flops 2147483648 | bytes 21233664 | tf_op jit(solution)/shard_map/ti,ibc->btc/dot_general | solution.py:67
  218.4 1.8 gather_fusion.3
  220.3 1.8 gather_fusion.4
  222.1 1.4 fusion.5
  223.5 82.4 %reduce-scatter.4.cloned.1.call-done = f32[128,1024]{1,0:T(8,128)} async-done(((f32[1024,1024]{1,0:T(8,128)}), f32[128,1024]{1,0:T(8,128)}) %reduce-scatter.4.cloned.1.call-update) | async-done | bytes 524304 | tf_op jit(solution)/shard_map/reduce_scatter | solution.py:104
  306.0 2.1 fusion.4
  (56 shorter events, 0.5 us)
Async XLA Ops:
  8.0 1.5 copy-start
  8.0 55.5 %reduce-scatter.8.cloned.1.call-start = ((), (), s32[]{:S(2)}) async-start(), calls=%async_computation.9 | async-start | bytes 1572864 | tf_op jit(solution)/shard_map/reduce_scatter | solution.py:129
  57.7 103.2 %copy-start.3 = (f32[1,16,8192]{2,1,0:T(8,128)S(1)}, f32[1,16,8192]{2,1,0:T(8,128)}, u32[]{:S(2)}) copy-start(f32[1,16,8192]{2,1,0:T(8,128)} %param.21) | copy-start | bytes 1572868
  57.7 103.2 %copy-start.4 = (f32[1,16,8192]{2,1,0:T(8,128)S(1)}, f32[1,16,8192]{2,1,0:T(8,128)}, u32[]{:S(2)}) copy-start(f32[1,16,8192]{2,1,0:T(8,128)} %param.23) | copy-start | bytes 1572868
  57.7 17.7 %reduce-scatter.6.cloned.1.call-start = ((), (), s32[]{:S(2)}) async-start(), calls=%async_computation.8 | async-start | bytes 1572864 | tf_op jit(solution)/shard_map/reduce_scatter | solution.py:128
  63.5 20.7 %all-to-all-start.1 = ((f32[8,16,1024]{2,1,0:T(8,128)}), f32[8,16,1024]{2,1,0:T(8,128)S(1)}, u32[]{:S(2)}, u32[]{:S(2)}) async-start(f32[8,16,1024]{2,1,0:T(8,128)} %reduce-scatter.8.cloned.1.call-done), calls=%async_computation.4 | async-start | bytes 1048576 | tf_op jit(solution)/shard_map/all_to_all | solution.py:133
  84.2 18.3 %all-to-all-start = ((f32[8,16,1024]{2,1,0:T(8,128)}), f32[8,16,1024]{2,1,0:T(8,128)S(1)}, u32[]{:S(2)}, u32[]{:S(2)}) async-start(f32[8,16,1024]{2,1,0:T(8,128)} %reduce-scatter.6.cloned.1.call-done), calls=%async_computation.2 | async-start | bytes 1048576 | tf_op jit(solution)/shard_map/all_to_all | solution.py:132
  156.8 18.0 %all-to-all-start.2 = ((f32[16,1,8192]{2,1,0:T(1,128)}), f32[16,1,8192]{2,1,0:T(1,128)S(1)}, u32[]{:S(2)}, u32[]{:S(2)}) async-start(f32[16,1,8192]{2,1,0:T(1,128)} %reshape.317), calls=%async_computation.5 | async-start | bytes 1048576 | tf_op jit(solution)/shard_map/all_to_all | solution.py:140
  160.5 57.9 %all-gather.5.cloned.1.call-start = ((), (), s32[]{:S(2)}) async-start(), calls=%async_computation.10 | async-start | bytes 1572864 | tf_op jit(solution)/shard_map/all_gather | solution.py:144
  186.0 32.3 %copy-start.6 = (s32[16]{0:T(128)S(1)}, s32[16]{0:T(128)}, u32[]{:S(2)}) copy-start(s32[16]{0:T(128)} %param.16) | copy-start | bytes 196
  189.5 32.6 %copy-start.1 = (bf16[16,16,1024]{2,1,0:T(8,128)(2,1)S(1)}, bf16[16,16,1024]{2,1,0:T(8,128)(2,1)}, u32[]{:S(2)}) copy-start(bf16[16,16,1024]{2,1,0:T(8,128)(2,1)} %param.19) | copy-start | bytes 1572868
  189.5 32.7 %copy-start.2 = (bf16[16,16,1024]{2,1,0:T(8,128)(2,1)S(1)}, bf16[16,16,1024]{2,1,0:T(8,128)(2,1)}, u32[]{:S(2)}) copy-start(bf16[16,16,1024]{2,1,0:T(8,128)(2,1)} %param.18) | copy-start | bytes 1572868
  189.5 30.8 %all-gather.7.cloned.1.call-start = ((), (), s32[]{:S(2)}) async-start(), calls=%async_computation.11 | async-start | bytes 1572864 | tf_op jit(solution)/shard_map/all_gather | solution.py:145
  208.1 97.9 %reduce-scatter.4.cloned.1.call-start = ((), (), s32[]{:S(2)}) async-start(), calls=%async_computation.7 | async-start | bytes 4718592 | tf_op jit(solution)/shard_map/reduce_scatter | solution.py:104
  208.1 97.9 %copy-start.5 = (s32[128]{0:T(128)S(1)}, s32[128]{0:T(128)}, u32[]{:S(2)}) copy-start(s32[128]{0:T(128)} %param.15) | copy-start | bytes 1540
Sparse Core Ops, SparseCore 0:
  57.8 5.6 reduce-scatter.7
  65.8 9.5 reduce-scatter.5
  189.6 8.5 all-gather.4
  208.2 8.4 all-gather.6
Sparse Core Ops, SparseCore 1:
  218.4 87.5 reduce-scatter.3
